TPU v7x, 256 devices: a whole 4x4x8 slice. The times are simulated.
256 devices in a mesh: ctx: 16 (over y_hi, x, core), dp: 16 (over y_lo, z).
Axes of the slice: x: 4, y: 4 (y_hi: 2, y_lo: 2; y = y_hi * 2 + y_lo), z: 8, core: 2. Of those that a mesh axis runs over, the one named last changes fastest.
Arguments:
- queries: bfloat16 [16, 2048, 1536], P('dp', 'ctx'), as said below
- keys: bfloat16 [16, 2048, 1536], P('dp', 'ctx'), as said below
- values: bfloat16 [16, 2048, 1536], P('dp', 'ctx'), may hold values from -6 to 6
- tangent_queries: bfloat16 [16, 2048, 1536], P('dp', 'ctx'), may hold values from -6 to 6
- tangent_keys: bfloat16 [16, 2048, 1536], P('dp', 'ctx'), may hold values from -6 to 6
- tangent_values: bfloat16 [16, 2048, 1536], P('dp', 'ctx'), may hold values from -6 to 6
- clip_ids: int32 [16, 2048], P('dp', 'ctx'), may hold values from 0 to 3, never falling along the last dimension, each value on 1 to 1024 neighbouring positions
- block_order: int32 [16], replicated, may hold values from 0 to 15, each once
- out_weight: bfloat16 [1536, 3072], replicated, may hold values from -0.15625 to 0.15625
- layer_scale: float32 [3072], replicated, may hold values from 0.1 to 1.9
- cotangent: bfloat16 [16, 2048, 3072], P('dp', 'ctx'), as said below
Outputs:
- tangent_branch: bfloat16 [16, 2048, 3072], P('dp', 'ctx')
- scale_grad: float32 [3072], replicated
Inputs may be any that keep to these rules, and one draw needn't show every extreme that they name: `clip_ids`: ids never fall along a sample's rows; each of the 4 clips is a run of consecutive rows. `block_order`: each block number appears once. `queries`: real-valued. `keys`: real-valued. `cotangent`: real-valued.
All inputs are finite; a program needn't handle non-finite values.
Results may differ from a plain program's by a relative error of at most 0.02.
The roundings to bfloat16 on the way count: a program that leaves them out, or rounds other values in their place, can miss the bound.
Values may be sent and summed in bfloat16 or wider, within the bound.
A program may use at most 192 MiB of HBM per device.

v0:
```python
import math
import jax
import jax.numpy as jnp
from jax import lax
from jax.sharding import PartitionSpec as P

HEADS = 12


def rotate(x, pos, half_dim):
    frequency = 10000.0 ** (-jnp.arange(half_dim, dtype=jnp.float32) / half_dim)
    angles = pos.astype(jnp.float32)[:, None] * frequency[None, :]
    cosine = jnp.cos(angles)[:, None, :]
    sine_part = jnp.sin(angles)[:, None, :]
    front_part = x[..., :half_dim]
    back_part = x[..., half_dim:]
    return jnp.concatenate(
        [front_part * cosine - back_part * sine_part, back_part * cosine + front_part * sine_part],
        axis=-1,
    )


def make_attend(query_rot, tquery_rot, query_ids, scale):

    def attend(carry, block):
        best, total, weighted, primal_acc, slope_acc, spread_acc = carry
        key_blk, value_blk, tkey_blk, tvalue_blk, key_ids = block
        scores = (
            jnp.einsum("hqd,hkd->hqk", query_rot, key_blk, preferred_element_type=jnp.float32)
            * scale
        )
        same_clip = query_ids[:, None] == key_ids[None, :]
        scores = jnp.where(same_clip[None], scores, -jnp.inf)
        slopes = (
            jnp.einsum("hqd,hkd->hqk", tquery_rot, key_blk, preferred_element_type=jnp.float32)
            + jnp.einsum("hqd,hkd->hqk", query_rot, tkey_blk, preferred_element_type=jnp.float32)
        ) * scale
        new_best = jnp.maximum(best, jnp.max(scores, axis=-1))
        factor = jnp.exp(best - new_best)
        weights = jnp.exp(scores - new_best[..., None])
        tilted = weights * slopes
        total = total * factor + jnp.sum(weights, axis=-1)
        weighted = weighted * factor + jnp.sum(tilted, axis=-1)
        weights_b = weights.astype(jnp.bfloat16)
        tilted_b = tilted.astype(jnp.bfloat16)
        primal_acc = primal_acc * factor[..., None] + jnp.einsum(
            "hqk,hkd->hqd", weights_b, value_blk, preferred_element_type=jnp.float32
        )
        slope_acc = slope_acc * factor[..., None] + jnp.einsum(
            "hqk,hkd->hqd", tilted_b, value_blk, preferred_element_type=jnp.float32
        )
        spread_acc = spread_acc * factor[..., None] + jnp.einsum(
            "hqk,hkd->hqd", weights_b, tvalue_blk, preferred_element_type=jnp.float32
        )
        return ((new_best, total, weighted, primal_acc, slope_acc, spread_acc), None)

    return attend


def start_states(heads, rows, head_dim):
    zeros_rows = jnp.zeros((heads, rows), jnp.float32)
    zeros_heads = jnp.zeros((heads, rows, head_dim), jnp.float32)
    return (
        jnp.full((heads, rows), -1e30, jnp.float32),
        zeros_rows,
        zeros_rows,
        zeros_heads,
        zeros_heads,
        zeros_heads,
    )


def local(
    queries,
    keys,
    values,
    tangent_queries,
    tangent_keys,
    tangent_values,
    clip_ids,
    block_order,
    out_weight,
    layer_scale,
    cotangent,
):
    tok_rows = queries.shape[1]
    heads = HEADS
    head_dim = queries.shape[2] // heads
    scale = head_dim ** (-0.5)
    cycle_index = lax.axis_index("ctx")
    positions = block_order[cycle_index] * tok_rows + jnp.arange(tok_rows, dtype=jnp.int32)

    def heads_first(x, turned):
        y = x[0].reshape(tok_rows, heads, head_dim)
        if turned:
            y = rotate(y.astype(jnp.float32), positions, head_dim // 2).astype(jnp.bfloat16)
        return jnp.transpose(y, (1, 0, 2))

    query_rot = heads_first(queries, True)
    key_rot = heads_first(keys, True)
    value_heads = heads_first(values, False)
    tquery_rot = heads_first(tangent_queries, True)
    tkey_rot = heads_first(tangent_keys, True)
    tvalue_heads = heads_first(tangent_values, False)
    all_ids = lax.all_gather(clip_ids, "ctx", axis=1, tiled=True)[0]
    own_ids = clip_ids[0]
    attend = make_attend(query_rot, tquery_rot, own_ids, scale)
    carry = start_states(heads, tok_rows, head_dim)
    key_part = lax.all_gather(key_rot, "ctx", axis=1, tiled=True)
    value_part = lax.all_gather(value_heads, "ctx", axis=1, tiled=True)
    tkey_part = lax.all_gather(tkey_rot, "ctx", axis=1, tiled=True)
    tvalue_part = lax.all_gather(tvalue_heads, "ctx", axis=1, tiled=True)
    count = key_part.shape[1]
    block_rows = math.gcd(count, tok_rows)
    blocks = count // block_rows

    def split_blocks(x):
        return jnp.transpose(x.reshape(heads, blocks, block_rows, head_dim), (1, 0, 2, 3))

    stacked = (
        split_blocks(key_part),
        split_blocks(value_part),
        split_blocks(tkey_part),
        split_blocks(tvalue_part),
        all_ids.reshape(blocks, block_rows),
    )
    carry, unused = lax.scan(attend, carry, stacked)
    best, total, weighted, primal_acc, slope_acc, spread_acc = carry
    mean_out = primal_acc / total[..., None]
    tangent_heads = (
        (slope_acc + spread_acc) / total[..., None] - (weighted / total)[..., None] * mean_out
    ).astype(jnp.bfloat16)
    tangent_rows = jnp.transpose(tangent_heads, (1, 0, 2)).reshape(tok_rows, heads * head_dim)
    projected = jnp.dot(tangent_rows, out_weight, preferred_element_type=jnp.float32)
    branch = (layer_scale * projected).astype(jnp.bfloat16)[None]
    partial_grad = jnp.sum(cotangent[0].astype(jnp.float32) * projected, axis=0)
    summed = lax.psum(partial_grad, ("ctx", "dp"))
    count_all = lax.axis_size("ctx") * lax.axis_size("dp") * tok_rows
    return (branch, summed / math.sqrt(count_all))


def solution(mesh):
    in_specs = (
        P("dp", "ctx", None),
        P("dp", "ctx", None),
        P("dp", "ctx", None),
        P("dp", "ctx", None),
        P("dp", "ctx", None),
        P("dp", "ctx", None),
        P("dp", "ctx"),
        P(),
        P(),
        P(),
        P("dp", "ctx", None),
    )
    out_specs = (P("dp", "ctx", None), P())
    return jax.shard_map(local, mesh=mesh, in_specs=in_specs, out_specs=out_specs, check_vma=False)
```

profile of v0, /device:TPU:1, one launch (start us, length us, event | category | flops | bytes accessed | tf_op | source)
XLA Modules:
  0.0 623.5 jit_solution(16415383374081786712)
XLA Ops:
  18.6 1.9 copy.28
  22.8 25.8 %all_gather.15 = s32[1,2048]{1,0:T(1,128)} all-gather(s32[1,128]{1,0:T(1,128)} %param.19), channel_id=1, replica_groups=mesh['ctx'=16,'dp'=16] {'ctx'}, dimensions={1}, use_global_device_ids=true | all-gather | bytes 8704 | tf_op jit(solution)/shard_map/all_gather | solution.py:105
  48.7 46.9 %all-gather.5.cloned.1.call-done = bf16[12,2048,128]{1,2,0:T(8,128)(2,1)} async-done(((bf16[12,128,128]{1,2,0:T(8,128)(2,1)}), bf16[12,2048,128]{1,2,0:T(8,128)(2,1)}) %all-gather.5.cloned.1.call-update) | async-done | bytes 6291472 | tf_op jit(solution)/shard_map/all_gather | solution.py:109
  95.6 7.8 %copy.44 = bf16[192,8,16,128]{3,2,1,0:T(8,128)(2,1)} copy(bf16[192,8,16,128]{3,1,2,0:T(8,128)(2,1)} %bitcast.120) | data formatting | bytes 12582912
  103.3 9.0 %copy.21 = bf16[12,16,128,128]{3,2,0,1:T(8,128)(2,1)} copy(bf16[12,16,128,128]{2,1,3,0:T(8,128)(2,1)} %bitcast.115) | data formatting | bytes 12582912 | tf_op jit(solution)/shard_map/reshape | solution.py:118
  112.4 58.9 %all-gather.7.cloned.1.call-done = bf16[12,2048,128]{1,2,0:T(8,128)(2,1)} async-done(((bf16[12,128,128]{1,2,0:T(8,128)(2,1)}), bf16[12,2048,128]{1,2,0:T(8,128)(2,1)}) %all-gather.7.cloned.1.call-update) | async-done | bytes 6291472 | tf_op jit(solution)/shard_map/all_gather | solution.py:111
  171.3 8.7 %copy.25 = bf16[12,2048,128]{2,1,0:T(8,128)(2,1)} copy(bf16[12,2048,128]{1,2,0:T(8,128)(2,1)} %all-gather.7.cloned.1.call-done) | data formatting | bytes 12582912 | tf_op jit(solution)/shard_map/all_gather | solution.py:111
  180.0 67.1 %all-gather.9.cloned.1.call-done = bf16[12,2048,128]{1,2,0:T(8,128)(2,1)} async-done(((bf16[12,128,128]{1,2,0:T(8,128)(2,1)}), bf16[12,2048,128]{1,2,0:T(8,128)(2,1)}) %all-gather.9.cloned.1.call-update) | async-done | bytes 6291472 | tf_op jit(solution)/shard_map/all_gather | solution.py:110
  247.1 8.6 %copy.27 = bf16[12,2048,128]{2,1,0:T(8,128)(2,1)} copy(bf16[12,2048,128]{1,2,0:T(8,128)(2,1)} %all-gather.9.cloned.1.call-done) | data formatting | bytes 12582912 | tf_op jit(solution)/shard_map/all_gather | solution.py:110
  255.7 67.0 %all-gather.11.cloned.1.call-done = bf16[12,2048,128]{1,2,0:T(8,128)(2,1)} async-done(((bf16[12,128,128]{1,2,0:T(8,128)(2,1)}), bf16[12,2048,128]{1,2,0:T(8,128)(2,1)}) %all-gather.11.cloned.1.call-update) | async-done | bytes 6291472 | tf_op jit(solution)/shard_map/all_gather | solution.py:112
  322.7 8.7 %copy.29 = bf16[12,2048,128]{2,1,0:T(8,128)(2,1)} copy(bf16[12,2048,128]{1,2,0:T(8,128)(2,1)} %all-gather.11.cloned.1.call-done) | data formatting | bytes 12582912 | tf_op jit(solution)/shard_map/all_gather | solution.py:112
  331.3 200.5 %while.21 = (s32[]{:T(128)}, f32[12,128]{1,0:T(8,128)S(1)}, f32[12,128]{1,0:T(8,128)}, f32[12,128]{1,0:T(8,128)}, f32[12,128,128]{2,1,0:T(8,128)S(1)}, /*index=5...) while((s32[]{:T(128)}, f32[12,128]{1,0:T(8,128)S(1)}, ...), condition=%wide.region_4.5_spmd.clone, body=%wide.region_0.4_spmd.clone.sunk | while | flops 306735616 | bytes 14789864 | solution.py:127
  353.5 1.6 convolution_add_fusion.7
  378.6 1.6 convolution_add_fusion.7
  403.8 1.6 convolution_add_fusion.7
  441.5 1.6 convolution_add_fusion.7
  454.1 1.6 convolution_add_fusion.7
  466.6 1.6 convolution_add_fusion.7
  491.8 1.6 convolution_add_fusion.7
  504.3 1.6 convolution_add_fusion.7
  516.9 1.6 convolution_add_fusion.7
  529.5 1.6 convolution_add_fusion.7
  534.3 6.4 %fusion.32 = (f32[3072]{0:T(1024)S(1)}, bf16[1,128,3072]{2,1,0:T(8,128)(2,1)}) fusion(bf16[1,128,3072]{2,1,0:T(8,128)(2,1)} %param.23, f32[3072]{0:T(1024)S(1)} %copy-done.3, bf16[128,1536]{0,1:T(8,128)(2,1)S(1)} %bitcast.121, bf16[1536,3072]{1,0:T(8,128)(2,1)} %param.21), kind=kOutput, calls=%fused_computation.46 | convolution fusion | flops 1209922560 | bytes 11427840 | tf_op jit(solution)/shard_map/dot_general | solution.py:134
  540.7 75.7 %psum.7 = f32[3072]{0:T(1024)S(1)} all-reduce(f32[3072]{0:T(1024)S(1)} %get-tuple-element.187), channel_id=1, replica_groups=mesh['ctx'=16,'dp'=16] {'ctx','dp'}, use_global_device_ids=true, to_apply=%region_6.7 | all-reduce | flops 3072 | bytes 24576 | tf_op jit(solution)/shard_map/psum | solution.py:137
  (305 shorter events, 198.9 us)
Async XLA Ops:
  7.2 88.4 %all-gather.5.cloned.1.call-start = ((), (), s32[]{:S(2)}) async-start(), calls=%async_computation | async-start | bytes 6684672 | tf_op jit(solution)/shard_map/all_gather | solution.py:109
  11.7 5.9 copy-start.2
  16.6 154.7 %all-gather.7.cloned.1.call-start = ((), (), s32[]{:S(2)}) async-start(), calls=%async_computation.1 | async-start | bytes 6684672 | tf_op jit(solution)/shard_map/all_gather | solution.py:111
  17.5 229.6 %all-gather.9.cloned.1.call-start = ((), (), s32[]{:S(2)}) async-start(), calls=%async_computation.2 | async-start | bytes 6684672 | tf_op jit(solution)/shard_map/all_gather | solution.py:110
  18.5 304.1 %all-gather.11.cloned.1.call-start = ((), (), s32[]{:S(2)}) async-start(), calls=%async_computation.3 | async-start | bytes 6684672 | tf_op jit(solution)/shard_map/all_gather | solution.py:112
  334.2 8.4 %copy-start = (f32[12,128]{1,0:T(8,128)S(1)}, f32[12,128]{1,0:T(8,128)}, u32[]{:S(2)}) copy-start(f32[12,128]{1,0:T(8,128)} %get-tuple-element.331) | copy-start | bytes 18436 | tf_op jit(solution)/shard_map/while
  346.1 9.1 %copy-start = (f32[12,128]{1,0:T(8,128)S(1)}, f32[12,128]{1,0:T(8,128)}, u32[]{:S(2)}) copy-start(f32[12,128]{1,0:T(8,128)} %get-tuple-element.331) | copy-start | bytes 18436 | tf_op jit(solution)/shard_map/while
  355.2 0.6 copy-start.1
  358.6 9.1 %copy-start = (f32[12,128]{1,0:T(8,128)S(1)}, f32[12,128]{1,0:T(8,128)}, u32[]{:S(2)}) copy-start(f32[12,128]{1,0:T(8,128)} %get-tuple-element.331) | copy-start | bytes 18436 | tf_op jit(solution)/shard_map/while
  367.8 0.6 copy-start.1
  371.2 9.1 %copy-start = (f32[12,128]{1,0:T(8,128)S(1)}, f32[12,128]{1,0:T(8,128)}, u32[]{:S(2)}) copy-start(f32[12,128]{1,0:T(8,128)} %get-tuple-element.331) | copy-start | bytes 18436 | tf_op jit(solution)/shard_map/while
  383.8 9.1 %copy-start = (f32[12,128]{1,0:T(8,128)S(1)}, f32[12,128]{1,0:T(8,128)}, u32[]{:S(2)}) copy-start(f32[12,128]{1,0:T(8,128)} %get-tuple-element.331) | copy-start | bytes 18436 | tf_op jit(solution)/shard_map/while
  396.4 9.1 %copy-start = (f32[12,128]{1,0:T(8,128)S(1)}, f32[12,128]{1,0:T(8,128)}, u32[]{:S(2)}) copy-start(f32[12,128]{1,0:T(8,128)} %get-tuple-element.331) | copy-start | bytes 18436 | tf_op jit(solution)/shard_map/while
  408.9 9.1 %copy-start = (f32[12,128]{1,0:T(8,128)S(1)}, f32[12,128]{1,0:T(8,128)}, u32[]{:S(2)}) copy-start(f32[12,128]{1,0:T(8,128)} %get-tuple-element.331) | copy-start | bytes 18436 | tf_op jit(solution)/shard_map/while
  421.5 9.1 %copy-start = (f32[12,128]{1,0:T(8,128)S(1)}, f32[12,128]{1,0:T(8,128)}, u32[]{:S(2)}) copy-start(f32[12,128]{1,0:T(8,128)} %get-tuple-element.331) | copy-start | bytes 18436 | tf_op jit(solution)/shard_map/while
  434.1 9.1 %copy-start = (f32[12,128]{1,0:T(8,128)S(1)}, f32[12,128]{1,0:T(8,128)}, u32[]{:S(2)}) copy-start(f32[12,128]{1,0:T(8,128)} %get-tuple-element.331) | copy-start | bytes 18436 | tf_op jit(solution)/shard_map/while
  446.7 9.1 %copy-start = (f32[12,128]{1,0:T(8,128)S(1)}, f32[12,128]{1,0:T(8,128)}, u32[]{:S(2)}) copy-start(f32[12,128]{1,0:T(8,128)} %get-tuple-element.331) | copy-start | bytes 18436 | tf_op jit(solution)/shard_map/while
  459.2 9.1 %copy-start = (f32[12,128]{1,0:T(8,128)S(1)}, f32[12,128]{1,0:T(8,128)}, u32[]{:S(2)}) copy-start(f32[12,128]{1,0:T(8,128)} %get-tuple-element.331) | copy-start | bytes 18436 | tf_op jit(solution)/shard_map/while
  471.8 9.1 %copy-start = (f32[12,128]{1,0:T(8,128)S(1)}, f32[12,128]{1,0:T(8,128)}, u32[]{:S(2)}) copy-start(f32[12,128]{1,0:T(8,128)} %get-tuple-element.331) | copy-start | bytes 18436 | tf_op jit(solution)/shard_map/while
  484.4 9.1 %copy-start = (f32[12,128]{1,0:T(8,128)S(1)}, f32[12,128]{1,0:T(8,128)}, u32[]{:S(2)}) copy-start(f32[12,128]{1,0:T(8,128)} %get-tuple-element.331) | copy-start | bytes 18436 | tf_op jit(solution)/shard_map/while
  496.9 9.1 %copy-start = (f32[12,128]{1,0:T(8,128)S(1)}, f32[12,128]{1,0:T(8,128)}, u32[]{:S(2)}) copy-start(f32[12,128]{1,0:T(8,128)} %get-tuple-element.331) | copy-start | bytes 18436 | tf_op jit(solution)/shard_map/while
  509.5 9.1 %copy-start = (f32[12,128]{1,0:T(8,128)S(1)}, f32[12,128]{1,0:T(8,128)}, u32[]{:S(2)}) copy-start(f32[12,128]{1,0:T(8,128)} %get-tuple-element.331) | copy-start | bytes 18436 | tf_op jit(solution)/shard_map/while
  522.1 9.1 %copy-start = (f32[12,128]{1,0:T(8,128)S(1)}, f32[12,128]{1,0:T(8,128)}, u32[]{:S(2)}) copy-start(f32[12,128]{1,0:T(8,128)} %get-tuple-element.331) | copy-start | bytes 18436 | tf_op jit(solution)/shard_map/while
  531.8 2.5 copy-start.3
  (14 other events, 8.4 us)
Sparse Core Ops, SparseCore 0:
  16.7 78.7 all-gather.4
  98.1 73.1 all-gather.6
  173.9 73.1 all-gather.8
  249.5 73.1 all-gather.10
where the time goes:
time: 630 us; the launch traced here: 623 us
  waiting for transfers between devices  240 us (38%)
  matrix products  150 us (24%)
  blocking collectives  102 us (16%)
  local copies, waits for them, and re-layouts  74 us (12%)
  other arithmetic  41 us (7%)
  between operations  14.6 us (2%)
    psum x1, blocking collectives, local(): summed = lax.psum(partial_grad, ('ctx', 'dp'))  75.7 us
    all_gather x1, waiting for transfers between devices, local(): value_part = lax.all_gather(value_heads, 'ctx', axis=1, tiled=True)  67.1 us
    all_gather x1, waiting for transfers between devices, local(): tvalue_part = lax.all_gather(tvalue_heads, 'ctx', axis=1, tiled=True)  67 us
    all_gather x1, waiting for transfers between devices, local(): tkey_part = lax.all_gather(tkey_rot, 'ctx', axis=1, tiled=True)  58.9 us
    all_gather x1, waiting for transfers between devices, local(): key_part = lax.all_gather(key_rot, 'ctx', axis=1, tiled=True)  46.9 us
    all_gather x1, blocking collectives, local(): all_ids = lax.all_gather(clip_ids, 'ctx', axis=1, tiled=True)[0]  25.8 us
    dot_general x16, matrix products, attend(): jnp.einsum('hqk,hkd->hqd', weights_b, value_blk, preferred_element_type=j...  25.1 us
    dot_general x16, matrix products, attend(): jnp.einsum('hqk,hkd->hqd', tilted_b, value_blk, preferred_element_type=jn...  24.9 us
  transfers between devices with their start and end apart: 4, of which 4 were waited for; matrix products, arithmetic and copies ran while one was open for 6% of the time, Pallas kernels for 0%

commit v1 on v0

--- a/solution.py
+++ b/solution.py
@@ -134,7 +134,7 @@
     projected = jnp.dot(tangent_rows, out_weight, preferred_element_type=jnp.float32)
     branch = (layer_scale * projected).astype(jnp.bfloat16)[None]
     partial_grad = jnp.sum(cotangent[0].astype(jnp.float32) * projected, axis=0)
-    summed = lax.psum(partial_grad, ("ctx", "dp"))
+    summed = lax.psum(lax.psum(partial_grad, "dp"), "ctx")
     count_all = lax.axis_size("ctx") * lax.axis_size("dp") * tok_rows
     return (branch, summed / math.sqrt(count_all))
 

time: 630 us -> 681 us (1.081)
  blocking collectives: 102 us -> 149 us
    psum x1 -> x2, blocking collectives: 75.7 us -> 122 us  [local(): summed = lax.psum(lax.psum(partial_grad, 'dp'), 'ctx')]
where the time goes in v1:
time: 681 us; the launch traced here: 670 us
  waiting for transfers between devices  239 us (35%)
  matrix products  150 us (22%)
  blocking collectives  149 us (22%)
  local copies, waits for them, and re-layouts  74.1 us (11%)
  other arithmetic  41 us (6%)
  between operations  14.6 us (2%)
    psum x2, blocking collectives, local(): summed = lax.psum(lax.psum(partial_grad, 'dp'), 'ctx')  122 us
    all_gather x1, waiting for transfers between devices, local(): value_part = lax.all_gather(value_heads, 'ctx', axis=1, tiled=True)  67.1 us
    all_gather x1, waiting for transfers between devices, local(): tvalue_part = lax.all_gather(tvalue_heads, 'ctx', axis=1, tiled=True)  67 us
    all_gather x1, waiting for transfers between devices, local(): tkey_part = lax.all_gather(tkey_rot, 'ctx', axis=1, tiled=True)  58.8 us
    all_gather x1, waiting for transfers between devices, local(): key_part = lax.all_gather(key_rot, 'ctx', axis=1, tiled=True)  46.3 us
    all_gather x1, blocking collectives, local(): all_ids = lax.all_gather(clip_ids, 'ctx', axis=1, tiled=True)[0]  26.4 us
    dot_general x16, matrix products, attend(): jnp.einsum('hqk,hkd->hqd', weights_b, value_blk, preferred_element_type=j...  25.1 us
    dot_general x16, matrix products, attend(): jnp.einsum('hqk,hkd->hqd', tilted_b, value_blk, preferred_element_type=jn...  24.9 us
  transfers between devices with their start and end apart: 4, of which 4 were waited for; matrix products, arithmetic and copies ran while one was open for 6% of the time, Pallas kernels for 0%

profile of v1, /device:TPU:1, one launch (start us, length us, event | category | flops | bytes accessed | tf_op | source)
XLA Modules:
  0.0 670.1 jit_solution(7012222902492231248)
XLA Ops:
  18.6 1.9 copy.28
  22.9 26.4 %all_gather.15 = s32[1,2048]{1,0:T(1,128)} all-gather(s32[1,128]{1,0:T(1,128)} %param.19), channel_id=1, replica_groups=mesh['ctx'=16,'dp'=16] {'ctx'}, dimensions={1}, use_global_device_ids=true | all-gather | bytes 8704 | tf_op jit(solution)/shard_map/all_gather | solution.py:105
  49.3 46.3 %all-gather.5.cloned.1.call-done = bf16[12,2048,128]{1,2,0:T(8,128)(2,1)} async-done(((bf16[12,128,128]{1,2,0:T(8,128)(2,1)}), bf16[12,2048,128]{1,2,0:T(8,128)(2,1)}) %all-gather.5.cloned.1.call-update) | async-done | bytes 6291472 | tf_op jit(solution)/shard_map/all_gather | solution.py:109
  95.6 7.8 %copy.44 = bf16[192,8,16,128]{3,2,1,0:T(8,128)(2,1)} copy(bf16[192,8,16,128]{3,1,2,0:T(8,128)(2,1)} %bitcast.120) | data formatting | bytes 12582912
  103.3 9.1 %copy.21 = bf16[12,16,128,128]{3,2,0,1:T(8,128)(2,1)} copy(bf16[12,16,128,128]{2,1,3,0:T(8,128)(2,1)} %bitcast.115) | data formatting | bytes 12582912 | tf_op jit(solution)/shard_map/reshape | solution.py:118
  112.5 58.8 %all-gather.7.cloned.1.call-done = bf16[12,2048,128]{1,2,0:T(8,128)(2,1)} async-done(((bf16[12,128,128]{1,2,0:T(8,128)(2,1)}), bf16[12,2048,128]{1,2,0:T(8,128)(2,1)}) %all-gather.7.cloned.1.call-update) | async-done | bytes 6291472 | tf_op jit(solution)/shard_map/all_gather | solution.py:111
  171.3 8.6 %copy.25 = bf16[12,2048,128]{2,1,0:T(8,128)(2,1)} copy(bf16[12,2048,128]{1,2,0:T(8,128)(2,1)} %all-gather.7.cloned.1.call-done) | data formatting | bytes 12582912 | tf_op jit(solution)/shard_map/all_gather | solution.py:111
  180.0 67.1 %all-gather.9.cloned.1.call-done = bf16[12,2048,128]{1,2,0:T(8,128)(2,1)} async-done(((bf16[12,128,128]{1,2,0:T(8,128)(2,1)}), bf16[12,2048,128]{1,2,0:T(8,128)(2,1)}) %all-gather.9.cloned.1.call-update) | async-done | bytes 6291472 | tf_op jit(solution)/shard_map/all_gather | solution.py:110
  247.1 8.6 %copy.27 = bf16[12,2048,128]{2,1,0:T(8,128)(2,1)} copy(bf16[12,2048,128]{1,2,0:T(8,128)(2,1)} %all-gather.9.cloned.1.call-done) | data formatting | bytes 12582912 | tf_op jit(solution)/shard_map/all_gather | solution.py:110
  255.7 67.0 %all-gather.11.cloned.1.call-done = bf16[12,2048,128]{1,2,0:T(8,128)(2,1)} async-done(((bf16[12,128,128]{1,2,0:T(8,128)(2,1)}), bf16[12,2048,128]{1,2,0:T(8,128)(2,1)}) %all-gather.11.cloned.1.call-update) | async-done | bytes 6291472 | tf_op jit(solution)/shard_map/all_gather | solution.py:112
  322.7 8.7 %copy.29 = bf16[12,2048,128]{2,1,0:T(8,128)(2,1)} copy(bf16[12,2048,128]{1,2,0:T(8,128)(2,1)} %all-gather.11.cloned.1.call-done) | data formatting | bytes 12582912 | tf_op jit(solution)/shard_map/all_gather | solution.py:112
  331.4 200.5 %while.21 = (s32[]{:T(128)}, f32[12,128]{1,0:T(8,128)S(1)}, f32[12,128]{1,0:T(8,128)}, f32[12,128]{1,0:T(8,128)}, f32[12,128,128]{2,1,0:T(8,128)S(1)}, /*index=5...) while((s32[]{:T(128)}, f32[12,128]{1,0:T(8,128)S(1)}, ...), condition=%wide.region_4.5_spmd.clone, body=%wide.region_0.4_spmd.clone.sunk | while | flops 306735616 | bytes 14789864 | solution.py:127
  353.5 1.6 convolution_add_fusion.7
  378.6 1.6 convolution_add_fusion.7
  391.2 1.6 convolution_add_fusion.7
  416.4 1.6 convolution_add_fusion.7
  429.0 1.6 convolution_add_fusion.7
  454.1 1.6 convolution_add_fusion.7
  479.2 1.6 convolution_add_fusion.7
  504.4 1.6 convolution_add_fusion.7
  529.5 1.6 convolution_add_fusion.7
  534.3 6.4 fusion.32
  540.7 49.0 %psum.14 = f32[3072]{0:T(1024)S(1)} all-reduce(f32[3072]{0:T(1024)S(1)} %get-tuple-element.187), channel_id=1, replica_groups=mesh['ctx'=16,'dp'=16] {'dp'}, use_global_device_ids=true, to_apply=%region_6.7 | all-reduce | flops 3072 | bytes 24576 | tf_op jit(solution)/shard_map/psum | solution.py:137
  589.7 73.3 %psum.15 = f32[3072]{0:T(1024)S(1)} all-reduce(f32[3072]{0:T(1024)S(1)} %psum.14), channel_id=1, replica_groups=mesh['ctx'=16,'dp'=16] {'ctx'}, use_global_device_ids=true, to_apply=%region_7.8 | all-reduce | flops 3072 | bytes 24576 | tf_op jit(solution)/shard_map/psum | solution.py:137
  (306 shorter events, 200.5 us)
Async XLA Ops:
  7.2 88.4 %all-gather.5.cloned.1.call-start = ((), (), s32[]{:S(2)}) async-start(), calls=%async_computation | async-start | bytes 6684672 | tf_op jit(solution)/shard_map/all_gather | solution.py:109
  11.7 5.9 copy-start.2
  16.6 154.7 %all-gather.7.cloned.1.call-start = ((), (), s32[]{:S(2)}) async-start(), calls=%async_computation.1 | async-start | bytes 6684672 | tf_op jit(solution)/shard_map/all_gather | solution.py:111
  17.5 229.6 %all-gather.9.cloned.1.call-start = ((), (), s32[]{:S(2)}) async-start(), calls=%async_computation.2 | async-start | bytes 6684672 | tf_op jit(solution)/shard_map/all_gather | solution.py:110
  18.5 304.2 %all-gather.11.cloned.1.call-start = ((), (), s32[]{:S(2)}) async-start(), calls=%async_computation.3 | async-start | bytes 6684672 | tf_op jit(solution)/shard_map/all_gather | solution.py:112
  334.2 8.4 %copy-start = (f32[12,128]{1,0:T(8,128)S(1)}, f32[12,128]{1,0:T(8,128)}, u32[]{:S(2)}) copy-start(f32[12,128]{1,0:T(8,128)} %get-tuple-element.331) | copy-start | bytes 18436 | tf_op jit(solution)/shard_map/while
  342.6 0.6 copy-start.1
  346.1 9.1 %copy-start = (f32[12,128]{1,0:T(8,128)S(1)}, f32[12,128]{1,0:T(8,128)}, u32[]{:S(2)}) copy-start(f32[12,128]{1,0:T(8,128)} %get-tuple-element.331) | copy-start | bytes 18436 | tf_op jit(solution)/shard_map/while
  358.7 9.1 %copy-start = (f32[12,128]{1,0:T(8,128)S(1)}, f32[12,128]{1,0:T(8,128)}, u32[]{:S(2)}) copy-start(f32[12,128]{1,0:T(8,128)} %get-tuple-element.331) | copy-start | bytes 18436 | tf_op jit(solution)/shard_map/while
  367.8 0.6 copy-start.1
  371.2 9.1 %copy-start = (f32[12,128]{1,0:T(8,128)S(1)}, f32[12,128]{1,0:T(8,128)}, u32[]{:S(2)}) copy-start(f32[12,128]{1,0:T(8,128)} %get-tuple-element.331) | copy-start | bytes 18436 | tf_op jit(solution)/shard_map/while
  383.8 9.1 %copy-start = (f32[12,128]{1,0:T(8,128)S(1)}, f32[12,128]{1,0:T(8,128)}, u32[]{:S(2)}) copy-start(f32[12,128]{1,0:T(8,128)} %get-tuple-element.331) | copy-start | bytes 18436 | tf_op jit(solution)/shard_map/while
  396.4 9.1 %copy-start = (f32[12,128]{1,0:T(8,128)S(1)}, f32[12,128]{1,0:T(8,128)}, u32[]{:S(2)}) copy-start(f32[12,128]{1,0:T(8,128)} %get-tuple-element.331) | copy-start | bytes 18436 | tf_op jit(solution)/shard_map/while
  409.0 9.1 %copy-start = (f32[12,128]{1,0:T(8,128)S(1)}, f32[12,128]{1,0:T(8,128)}, u32[]{:S(2)}) copy-start(f32[12,128]{1,0:T(8,128)} %get-tuple-element.331) | copy-start | bytes 18436 | tf_op jit(solution)/shard_map/while
  421.6 9.1 %copy-start = (f32[12,128]{1,0:T(8,128)S(1)}, f32[12,128]{1,0:T(8,128)}, u32[]{:S(2)}) copy-start(f32[12,128]{1,0:T(8,128)} %get-tuple-element.331) | copy-start | bytes 18436 | tf_op jit(solution)/shard_map/while
  434.1 9.1 %copy-start = (f32[12,128]{1,0:T(8,128)S(1)}, f32[12,128]{1,0:T(8,128)}, u32[]{:S(2)}) copy-start(f32[12,128]{1,0:T(8,128)} %get-tuple-element.331) | copy-start | bytes 18436 | tf_op jit(solution)/shard_map/while
  446.7 9.1 %copy-start = (f32[12,128]{1,0:T(8,128)S(1)}, f32[12,128]{1,0:T(8,128)}, u32[]{:S(2)}) copy-start(f32[12,128]{1,0:T(8,128)} %get-tuple-element.331) | copy-start | bytes 18436 | tf_op jit(solution)/shard_map/while
  459.3 9.1 %copy-start = (f32[12,128]{1,0:T(8,128)S(1)}, f32[12,128]{1,0:T(8,128)}, u32[]{:S(2)}) copy-start(f32[12,128]{1,0:T(8,128)} %get-tuple-element.331) | copy-start | bytes 18436 | tf_op jit(solution)/shard_map/while
  471.8 9.1 %copy-start = (f32[12,128]{1,0:T(8,128)S(1)}, f32[12,128]{1,0:T(8,128)}, u32[]{:S(2)}) copy-start(f32[12,128]{1,0:T(8,128)} %get-tuple-element.331) | copy-start | bytes 18436 | tf_op jit(solution)/shard_map/while
  484.4 9.1 %copy-start = (f32[12,128]{1,0:T(8,128)S(1)}, f32[12,128]{1,0:T(8,128)}, u32[]{:S(2)}) copy-start(f32[12,128]{1,0:T(8,128)} %get-tuple-element.331) | copy-start | bytes 18436 | tf_op jit(solution)/shard_map/while
  497.0 9.1 %copy-start = (f32[12,128]{1,0:T(8,128)S(1)}, f32[12,128]{1,0:T(8,128)}, u32[]{:S(2)}) copy-start(f32[12,128]{1,0:T(8,128)} %get-tuple-element.331) | copy-start | bytes 18436 | tf_op jit(solution)/shard_map/while
  509.5 9.1 %copy-start = (f32[12,128]{1,0:T(8,128)S(1)}, f32[12,128]{1,0:T(8,128)}, u32[]{:S(2)}) copy-start(f32[12,128]{1,0:T(8,128)} %get-tuple-element.331) | copy-start | bytes 18436 | tf_op jit(solution)/shard_map/while
  522.1 9.1 %copy-start = (f32[12,128]{1,0:T(8,128)S(1)}, f32[12,128]{1,0:T(8,128)}, u32[]{:S(2)}) copy-start(f32[12,128]{1,0:T(8,128)} %get-tuple-element.331) | copy-start | bytes 18436 | tf_op jit(solution)/shard_map/while
  531.8 2.5 copy-start.3
  (14 other events, 8.4 us)
Sparse Core Ops, SparseCore 0:
  16.7 78.7 all-gather.4
  98.1 73.1 all-gather.6
  173.9 73.1 all-gather.8
  249.5 73.1 all-gather.10
